TPU v7x, 256 devices: a whole 4x4x8 slice. The times are simulated.
256 devices in a mesh: state: 16 (over y_lo, x, core), mesh: 16 (over z, y_hi).
Axes of the slice: x: 4, y: 4 (y_hi: 2, y_lo: 2; y = y_hi * 2 + y_lo), z: 8, core: 2. Of those that a mesh axis runs over, the one named last changes fastest.
Arguments:
- states_in: float32 [22032, 4096], P('mesh', 'state'), may hold values from -6 to 6
- rotation: float32 [4096, 4096], P(None, 'state'), may hold values from -0.09375 to 0.09375
- stiffness: float32 [16, 729, 729], P('mesh'), as said below
- potential: float32 [22032], P('mesh'), may hold values from -1 to 1
- cell_nodes: int32 [32, 729], P('mesh'), may hold values from 0 to 1376, as said below
- shared_rows: int32 [64, 153], P('mesh'), may hold values from 0 to 1376, as said below
- shared_count: int32 [16, 4], P('mesh'), may hold values from 0 to 153, as said below
Outputs:
- filtered: float32 [22032, 4096], P('mesh', 'state')
Inputs may be any that keep to these rules, and one draw needn't show every extreme that they name: `cell_nodes`: each partition's 2 cells name its 1377 local nodes as a row of hexahedral cells of order 8 sharing faces; every local node is named by some cell. `shared_rows`: used rows name the partition's nodes on the face toward the partner, in the same geometric order as the partner's matching list; rows beyond the count name arbitrary local nodes. `shared_count`: count s of partition p equals count s ^ 1 of its partner; for s = 0, 1 it is 0 or from 40 to 81, for s = 2, 3 it is 0 or from 76 to 153; it is 0 where the partner lies outside the G by G grid; count 2 of partition 0 is 153. `stiffness`: symmetric with a diagonal of 1 to 3.
All inputs are finite; a program needn't handle non-finite values.
Results may differ from a plain program's by a relative error of at most 0.0001.
Values sent between devices are 32-bit elements; how exact they have to be, the bound alone decides.
No kernel may reach another device: no remote copies, remote signals or barrier semaphores. Data moves between devices by JAX's collectives and lax.ppermute only.
A program may use at most 64 MiB of HBM per device.

v0:
```python
import math

import jax
import jax.numpy as jnp
from jax import lax
from jax.sharding import PartitionSpec as P

center_shift = 3.0
half_width = 4.0


def from_behind(value, axis, by):
    count = lax.axis_size(axis)
    return lax.ppermute(value, axis, [(i, (i + by) % count) for i in range(count)])


def from_behind_2(value, axis, steps):
    count = lax.axis_size(axis)
    first, last = (max(0, -steps), min(count, count - steps))
    return lax.ppermute(value, axis, [(source, source + steps) for source in range(first, last)])


def matmul(left, right):
    return jnp.dot(left, right, precision=lax.Precision.HIGHEST, preferred_element_type=jnp.float32)


def per_device(states_in, rotation, stiffness, potential, cell_nodes, shared_rows, shared_count):
    block_cols = states_in.shape[1]
    count_state = lax.axis_size("state")
    own_index = lax.axis_index("state")

    def rows_of(block):
        return lax.dynamic_slice_in_dim(rotation, block * block_cols, block_cols, 0)

    def turn(step, carry):
        held, total = carry
        held = from_behind(held, "state", -1)
        block = (own_index + step) % count_state
        return (held, total + matmul(held, rows_of(block)))

    first = matmul(states_in, rows_of(own_index))
    held_last, rotated = lax.fori_loop(1, count_state, turn, (states_in, first))
    grid_side = math.isqrt(lax.axis_size("mesh"))
    row_mask = (jnp.arange(shared_rows.shape[1])[None, :] < shared_count[0][:, None]).astype(
        jnp.float32
    )

    def trade(values, send_slot, recv_slot, offset):
        block = values[shared_rows[send_slot]] * row_mask[send_slot][:, None]
        arrived = from_behind_2(block, "mesh", offset)
        return arrived * row_mask[recv_slot][:, None]

    def operator(field):
        gathered = field[cell_nodes]
        product = jnp.einsum("ij,cjs->cis", stiffness[0], gathered, precision=lax.Precision.HIGHEST)
        local = (
            jnp.zeros_like(field).at[cell_nodes.reshape(-1)].add(product.reshape(-1, block_cols))
        )
        from_next = trade(local, 1, 0, -grid_side)
        from_prev = trade(local, 0, 1, grid_side)
        sectioned = local.at[shared_rows[0]].add(from_next).at[shared_rows[1]].add(from_prev)
        from_right = trade(sectioned, 3, 2, -1)
        from_left = trade(sectioned, 2, 3, 1)
        assembled = sectioned.at[shared_rows[2]].add(from_right).at[shared_rows[3]].add(from_left)
        return assembled + potential[:, None] * field

    current = (operator(rotated) - center_shift * rotated) / half_width
    applied = operator(current)
    following = 2.0 * (applied - center_shift * current) / half_width - rotated
    return following


def solution(mesh):
    return jax.shard_map(
        per_device,
        mesh=mesh,
        in_specs=(
            P("mesh", "state"),
            P(None, "state"),
            P("mesh", None, None),
            P("mesh"),
            P("mesh", None),
            P("mesh", None),
            P("mesh", None),
        ),
        out_specs=P("mesh", "state"),
        check_vma=False,
    )
```

profile of v0, /device:TPU:64, one launch (start us, length us, event | category | flops | bytes accessed | tf_op | source)
XLA Modules:
  0.0 499.0 jit_solution(15673384634929503133)
XLA Ops:
  6.2 366.8 %while.17 = (s32[]{:T(128)}, f32[1377,256]{1,0:T(8,128)}, f32[1377,256]{1,0:T(8,128)S(1)}, s32[]{:T(128)}, f32[4096,256]{1,0:T(8,128)}, /*index=5*/s32[]{:T(128)...) while((s32[]{:T(128)}, f32[1377,256]{1,0:T(8,128)}, f32[1377,256]{1,0:T(8,128)S(1)}, ...), condition=%wide.region_1.2_spmd, body=%wide.region_0.1_spmd.sunk | while | flops 1083269376 | bytes 12952896 | solution.py:42
  9.5 16.6 %collective-permute-done = f32[1377,256]{1,0:T(8,128)S(1)} collective-permute-done((f32[1377,256]{1,0:T(8,128)}, f32[1377,256]{1,0:T(8,128)S(1)}, u32[]{:S(2)}, u32[]{:S(2)}) %collective-permute-start) | collective-permute-done | bytes 1410080 | tf_op jit(solution)/shard_map/while/body/eval_jaxpr/ppermute | solution.py:14
  34.0 16.6 %collective-permute-done = f32[1377,256]{1,0:T(8,128)S(1)} collective-permute-done((f32[1377,256]{1,0:T(8,128)}, f32[1377,256]{1,0:T(8,128)S(1)}, u32[]{:S(2)}, u32[]{:S(2)}) %collective-permute-start) | collective-permute-done | bytes 1410080 | tf_op jit(solution)/shard_map/while/body/eval_jaxpr/ppermute | solution.py:14
  58.5 16.6 %collective-permute-done = f32[1377,256]{1,0:T(8,128)S(1)} collective-permute-done((f32[1377,256]{1,0:T(8,128)}, f32[1377,256]{1,0:T(8,128)S(1)}, u32[]{:S(2)}, u32[]{:S(2)}) %collective-permute-start) | collective-permute-done | bytes 1410080 | tf_op jit(solution)/shard_map/while/body/eval_jaxpr/ppermute | solution.py:14
  83.0 16.6 %collective-permute-done = f32[1377,256]{1,0:T(8,128)S(1)} collective-permute-done((f32[1377,256]{1,0:T(8,128)}, f32[1377,256]{1,0:T(8,128)S(1)}, u32[]{:S(2)}, u32[]{:S(2)}) %collective-permute-start) | collective-permute-done | bytes 1410080 | tf_op jit(solution)/shard_map/while/body/eval_jaxpr/ppermute | solution.py:14
  107.5 16.6 %collective-permute-done = f32[1377,256]{1,0:T(8,128)S(1)} collective-permute-done((f32[1377,256]{1,0:T(8,128)}, f32[1377,256]{1,0:T(8,128)S(1)}, u32[]{:S(2)}, u32[]{:S(2)}) %collective-permute-start) | collective-permute-done | bytes 1410080 | tf_op jit(solution)/shard_map/while/body/eval_jaxpr/ppermute | solution.py:14
  132.0 16.6 %collective-permute-done = f32[1377,256]{1,0:T(8,128)S(1)} collective-permute-done((f32[1377,256]{1,0:T(8,128)}, f32[1377,256]{1,0:T(8,128)S(1)}, u32[]{:S(2)}, u32[]{:S(2)}) %collective-permute-start) | collective-permute-done | bytes 1410080 | tf_op jit(solution)/shard_map/while/body/eval_jaxpr/ppermute | solution.py:14
  156.5 16.6 %collective-permute-done = f32[1377,256]{1,0:T(8,128)S(1)} collective-permute-done((f32[1377,256]{1,0:T(8,128)}, f32[1377,256]{1,0:T(8,128)S(1)}, u32[]{:S(2)}, u32[]{:S(2)}) %collective-permute-start) | collective-permute-done | bytes 1410080 | tf_op jit(solution)/shard_map/while/body/eval_jaxpr/ppermute | solution.py:14
  181.1 16.6 %collective-permute-done = f32[1377,256]{1,0:T(8,128)S(1)} collective-permute-done((f32[1377,256]{1,0:T(8,128)}, f32[1377,256]{1,0:T(8,128)S(1)}, u32[]{:S(2)}, u32[]{:S(2)}) %collective-permute-start) | collective-permute-done | bytes 1410080 | tf_op jit(solution)/shard_map/while/body/eval_jaxpr/ppermute | solution.py:14
  205.6 16.6 %collective-permute-done = f32[1377,256]{1,0:T(8,128)S(1)} collective-permute-done((f32[1377,256]{1,0:T(8,128)}, f32[1377,256]{1,0:T(8,128)S(1)}, u32[]{:S(2)}, u32[]{:S(2)}) %collective-permute-start) | collective-permute-done | bytes 1410080 | tf_op jit(solution)/shard_map/while/body/eval_jaxpr/ppermute | solution.py:14
  230.1 16.6 %collective-permute-done = f32[1377,256]{1,0:T(8,128)S(1)} collective-permute-done((f32[1377,256]{1,0:T(8,128)}, f32[1377,256]{1,0:T(8,128)S(1)}, u32[]{:S(2)}, u32[]{:S(2)}) %collective-permute-start) | collective-permute-done | bytes 1410080 | tf_op jit(solution)/shard_map/while/body/eval_jaxpr/ppermute | solution.py:14
  254.6 16.6 %collective-permute-done = f32[1377,256]{1,0:T(8,128)S(1)} collective-permute-done((f32[1377,256]{1,0:T(8,128)}, f32[1377,256]{1,0:T(8,128)S(1)}, u32[]{:S(2)}, u32[]{:S(2)}) %collective-permute-start) | collective-permute-done | bytes 1410080 | tf_op jit(solution)/shard_map/while/body/eval_jaxpr/ppermute | solution.py:14
  279.1 16.6 %collective-permute-done = f32[1377,256]{1,0:T(8,128)S(1)} collective-permute-done((f32[1377,256]{1,0:T(8,128)}, f32[1377,256]{1,0:T(8,128)S(1)}, u32[]{:S(2)}, u32[]{:S(2)}) %collective-permute-start) | collective-permute-done | bytes 1410080 | tf_op jit(solution)/shard_map/while/body/eval_jaxpr/ppermute | solution.py:14
  303.6 16.6 %collective-permute-done = f32[1377,256]{1,0:T(8,128)S(1)} collective-permute-done((f32[1377,256]{1,0:T(8,128)}, f32[1377,256]{1,0:T(8,128)S(1)}, u32[]{:S(2)}, u32[]{:S(2)}) %collective-permute-start) | collective-permute-done | bytes 1410080 | tf_op jit(solution)/shard_map/while/body/eval_jaxpr/ppermute | solution.py:14
  328.1 16.6 %collective-permute-done = f32[1377,256]{1,0:T(8,128)S(1)} collective-permute-done((f32[1377,256]{1,0:T(8,128)}, f32[1377,256]{1,0:T(8,128)S(1)}, u32[]{:S(2)}, u32[]{:S(2)}) %collective-permute-start) | collective-permute-done | bytes 1410080 | tf_op jit(solution)/shard_map/while/body/eval_jaxpr/ppermute | solution.py:14
  352.6 16.6 %collective-permute-done = f32[1377,256]{1,0:T(8,128)S(1)} collective-permute-done((f32[1377,256]{1,0:T(8,128)}, f32[1377,256]{1,0:T(8,128)S(1)}, u32[]{:S(2)}, u32[]{:S(2)}) %collective-permute-start) | collective-permute-done | bytes 1410080 | tf_op jit(solution)/shard_map/while/body/eval_jaxpr/ppermute | solution.py:14
  378.2 5.8 %fusion.9 = f32[2,729,256]{2,1,0:T(8,128)S(1)} fusion(f32[2,729,256]{2,1,0:T(8,128)} %reshape.160, f32[1,729,729]{2,0,1:T(1,128)} %param.11), kind=kOutput, calls=%fused_computation.31 | convolution fusion | flops 3265173504 | bytes 5111748 | tf_op jit(solution)/shard_map/ij,cjs->cis/dot_general | solution.py:55
  385.4 9.0 %scatter_custom_fusion = f32[1377,256]{1,0:T(8,128)S(1)} fusion(s32[1458]{0:T(1024)S(1)} %fusion.44, f32[1458,256]{1,0:T(8,128)} %reshape.243, f32[]{:T(128)} %constant.84.clone.1), kind=kCustom, calls=%fused_computation.40 | custom fusion | flops 373248 | bytes 1410560 | tf_op jit(solution)/shard_map/scatter-add | solution.py:57
  398.1 6.4 %collective-permute-start.2 = (f32[153,256]{1,0:T(8,128)S(1)}, f32[153,256]{1,0:T(8,128)S(1)}, u32[]{:S(2)}, u32[]{:S(2)}) collective-permute-start(f32[153,256]{1,0:T(8,128)S(1)} %broadcast_multiply_fusion.6), channel_id=1, source_target_pairs={{0,4},{1,5},{2,6},{3,7},{4,8},{5,9},{6,10},{7,11},{8,12},{9,13},{1... | collective-permute-start | bytes 470024 | tf_op jit(solution)/shard_map/ppermute | solution.py:20
  416.3 5.4 %collective-permute-start.4 = (f32[153,256]{1,0:T(8,128)S(1)}, f32[153,256]{1,0:T(8,128)S(1)}, u32[]{:S(2)}, u32[]{:S(2)}) collective-permute-start(f32[153,256]{1,0:T(8,128)S(1)} %broadcast_multiply_fusion.2), channel_id=1, source_target_pairs={{0,1},{1,2},{2,3},{3,4},{4,5},{5,6},{6,7},{7,8},{8,9},{9,10},{10,1... | collective-permute-start | bytes 470024 | tf_op jit(solution)/shard_map/ppermute | solution.py:20
  438.4 6.5 %fusion.12 = f32[2,729,256]{2,1,0:T(8,128)} fusion(f32[2,729,256]{2,1,0:T(8,128)S(1)} %reshape.200, f32[1,729,729]{2,0,1:T(1,128)} %param.11), kind=kOutput, calls=%fused_computation.32 | convolution fusion | flops 3265173504 | bytes 5111748 | tf_op jit(solution)/shard_map/ij,cjs->cis/dot_general | solution.py:55
  447.6 8.8 %scatter_custom_fusion.5 = f32[1377,256]{1,0:T(8,128)S(1)} fusion(s32[1458]{0:T(1024)S(1)} %fusion.44, f32[1458,256]{1,0:T(8,128)} %reshape.283, f32[]{:T(128)} %constant.84.clone.1), kind=kCustom, calls=%fused_computation.38 | custom fusion | flops 373248 | bytes 1410560 | tf_op jit(solution)/shard_map/scatter-add | solution.py:57
  460.1 7.4 %collective-permute-start.6 = (f32[153,256]{1,0:T(8,128)S(1)}, f32[153,256]{1,0:T(8,128)S(1)}, u32[]{:S(2)}, u32[]{:S(2)}) collective-permute-start(f32[153,256]{1,0:T(8,128)S(1)} %broadcast_multiply_fusion.5), channel_id=1, source_target_pairs={{0,4},{1,5},{2,6},{3,7},{4,8},{5,9},{6,10},{7,11},{8,12},{9,13},{1... | collective-permute-start | bytes 470024 | tf_op jit(solution)/shard_map/ppermute | solution.py:20
  480.1 5.4 %collective-permute-start.8 = (f32[153,256]{1,0:T(8,128)S(1)}, f32[153,256]{1,0:T(8,128)S(1)}, u32[]{:S(2)}, u32[]{:S(2)}) collective-permute-start(f32[153,256]{1,0:T(8,128)S(1)} %broadcast_multiply_fusion.1), channel_id=1, source_target_pairs={{0,1},{1,2},{2,3},{3,4},{4,5},{5,6},{6,7},{7,8},{8,9},{9,10},{10,1... | collective-permute-start | bytes 470024 | tf_op jit(solution)/shard_map/ppermute | solution.py:20
  (120 shorter events, 194.7 us)
Async XLA Ops:
  2.8 394.4 %copy-start.5 = (s32[153,1]{0,1:T(1,128)}, s32[153,1]{0,1:T(1,128)S(1)}, u32[]{:S(2)}) copy-start(s32[153,1]{0,1:T(1,128)S(1)} %get-tuple-element.155) | copy-start | bytes 1840
  6.2 19.9 %collective-permute-start = (f32[1377,256]{1,0:T(8,128)}, f32[1377,256]{1,0:T(8,128)S(1)}, u32[]{:S(2)}, u32[]{:S(2)}) collective-permute-start(f32[1377,256]{1,0:T(8,128)} %get-tuple-element.200), channel_id=1, source_target_pairs={{0,240},{16,0},{32,16},{48,32},{64,48},{80,64},{96,80},{112,96},{1... | collective-permute-start | bytes 4230152 | tf_op jit(solution)/shard_map/while/body/eval_jaxpr/ppermute | solution.py:14
  30.0 20.6 %collective-permute-start = (f32[1377,256]{1,0:T(8,128)}, f32[1377,256]{1,0:T(8,128)S(1)}, u32[]{:S(2)}, u32[]{:S(2)}) collective-permute-start(f32[1377,256]{1,0:T(8,128)} %get-tuple-element.200), channel_id=1, source_target_pairs={{0,240},{16,0},{32,16},{48,32},{64,48},{80,64},{96,80},{112,96},{1... | collective-permute-start | bytes 4230152 | tf_op jit(solution)/shard_map/while/body/eval_jaxpr/ppermute | solution.py:14
  54.5 20.6 %collective-permute-start = (f32[1377,256]{1,0:T(8,128)}, f32[1377,256]{1,0:T(8,128)S(1)}, u32[]{:S(2)}, u32[]{:S(2)}) collective-permute-start(f32[1377,256]{1,0:T(8,128)} %get-tuple-element.200), channel_id=1, source_target_pairs={{0,240},{16,0},{32,16},{48,32},{64,48},{80,64},{96,80},{112,96},{1... | collective-permute-start | bytes 4230152 | tf_op jit(solution)/shard_map/while/body/eval_jaxpr/ppermute | solution.py:14
  79.0 20.6 %collective-permute-start = (f32[1377,256]{1,0:T(8,128)}, f32[1377,256]{1,0:T(8,128)S(1)}, u32[]{:S(2)}, u32[]{:S(2)}) collective-permute-start(f32[1377,256]{1,0:T(8,128)} %get-tuple-element.200), channel_id=1, source_target_pairs={{0,240},{16,0},{32,16},{48,32},{64,48},{80,64},{96,80},{112,96},{1... | collective-permute-start | bytes 4230152 | tf_op jit(solution)/shard_map/while/body/eval_jaxpr/ppermute | solution.py:14
  103.5 20.6 %collective-permute-start = (f32[1377,256]{1,0:T(8,128)}, f32[1377,256]{1,0:T(8,128)S(1)}, u32[]{:S(2)}, u32[]{:S(2)}) collective-permute-start(f32[1377,256]{1,0:T(8,128)} %get-tuple-element.200), channel_id=1, source_target_pairs={{0,240},{16,0},{32,16},{48,32},{64,48},{80,64},{96,80},{112,96},{1... | collective-permute-start | bytes 4230152 | tf_op jit(solution)/shard_map/while/body/eval_jaxpr/ppermute | solution.py:14
  128.1 20.6 %collective-permute-start = (f32[1377,256]{1,0:T(8,128)}, f32[1377,256]{1,0:T(8,128)S(1)}, u32[]{:S(2)}, u32[]{:S(2)}) collective-permute-start(f32[1377,256]{1,0:T(8,128)} %get-tuple-element.200), channel_id=1, source_target_pairs={{0,240},{16,0},{32,16},{48,32},{64,48},{80,64},{96,80},{112,96},{1... | collective-permute-start | bytes 4230152 | tf_op jit(solution)/shard_map/while/body/eval_jaxpr/ppermute | solution.py:14
  152.6 20.6 %collective-permute-start = (f32[1377,256]{1,0:T(8,128)}, f32[1377,256]{1,0:T(8,128)S(1)}, u32[]{:S(2)}, u32[]{:S(2)}) collective-permute-start(f32[1377,256]{1,0:T(8,128)} %get-tuple-element.200), channel_id=1, source_target_pairs={{0,240},{16,0},{32,16},{48,32},{64,48},{80,64},{96,80},{112,96},{1... | collective-permute-start | bytes 4230152 | tf_op jit(solution)/shard_map/while/body/eval_jaxpr/ppermute | solution.py:14
  177.1 20.6 %collective-permute-start = (f32[1377,256]{1,0:T(8,128)}, f32[1377,256]{1,0:T(8,128)S(1)}, u32[]{:S(2)}, u32[]{:S(2)}) collective-permute-start(f32[1377,256]{1,0:T(8,128)} %get-tuple-element.200), channel_id=1, source_target_pairs={{0,240},{16,0},{32,16},{48,32},{64,48},{80,64},{96,80},{112,96},{1... | collective-permute-start | bytes 4230152 | tf_op jit(solution)/shard_map/while/body/eval_jaxpr/ppermute | solution.py:14
  201.6 20.6 %collective-permute-start = (f32[1377,256]{1,0:T(8,128)}, f32[1377,256]{1,0:T(8,128)S(1)}, u32[]{:S(2)}, u32[]{:S(2)}) collective-permute-start(f32[1377,256]{1,0:T(8,128)} %get-tuple-element.200), channel_id=1, source_target_pairs={{0,240},{16,0},{32,16},{48,32},{64,48},{80,64},{96,80},{112,96},{1... | collective-permute-start | bytes 4230152 | tf_op jit(solution)/shard_map/while/body/eval_jaxpr/ppermute | solution.py:14
  226.1 20.6 %collective-permute-start = (f32[1377,256]{1,0:T(8,128)}, f32[1377,256]{1,0:T(8,128)S(1)}, u32[]{:S(2)}, u32[]{:S(2)}) collective-permute-start(f32[1377,256]{1,0:T(8,128)} %get-tuple-element.200), channel_id=1, source_target_pairs={{0,240},{16,0},{32,16},{48,32},{64,48},{80,64},{96,80},{112,96},{1... | collective-permute-start | bytes 4230152 | tf_op jit(solution)/shard_map/while/body/eval_jaxpr/ppermute | solution.py:14
  250.6 20.6 %collective-permute-start = (f32[1377,256]{1,0:T(8,128)}, f32[1377,256]{1,0:T(8,128)S(1)}, u32[]{:S(2)}, u32[]{:S(2)}) collective-permute-start(f32[1377,256]{1,0:T(8,128)} %get-tuple-element.200), channel_id=1, source_target_pairs={{0,240},{16,0},{32,16},{48,32},{64,48},{80,64},{96,80},{112,96},{1... | collective-permute-start | bytes 4230152 | tf_op jit(solution)/shard_map/while/body/eval_jaxpr/ppermute | solution.py:14
  275.1 20.6 %collective-permute-start = (f32[1377,256]{1,0:T(8,128)}, f32[1377,256]{1,0:T(8,128)S(1)}, u32[]{:S(2)}, u32[]{:S(2)}) collective-permute-start(f32[1377,256]{1,0:T(8,128)} %get-tuple-element.200), channel_id=1, source_target_pairs={{0,240},{16,0},{32,16},{48,32},{64,48},{80,64},{96,80},{112,96},{1... | collective-permute-start | bytes 4230152 | tf_op jit(solution)/shard_map/while/body/eval_jaxpr/ppermute | solution.py:14
  299.6 20.6 %collective-permute-start = (f32[1377,256]{1,0:T(8,128)}, f32[1377,256]{1,0:T(8,128)S(1)}, u32[]{:S(2)}, u32[]{:S(2)}) collective-permute-start(f32[1377,256]{1,0:T(8,128)} %get-tuple-element.200), channel_id=1, source_target_pairs={{0,240},{16,0},{32,16},{48,32},{64,48},{80,64},{96,80},{112,96},{1... | collective-permute-start | bytes 4230152 | tf_op jit(solution)/shard_map/while/body/eval_jaxpr/ppermute | solution.py:14
  324.1 20.6 %collective-permute-start = (f32[1377,256]{1,0:T(8,128)}, f32[1377,256]{1,0:T(8,128)S(1)}, u32[]{:S(2)}, u32[]{:S(2)}) collective-permute-start(f32[1377,256]{1,0:T(8,128)} %get-tuple-element.200), channel_id=1, source_target_pairs={{0,240},{16,0},{32,16},{48,32},{64,48},{80,64},{96,80},{112,96},{1... | collective-permute-start | bytes 4230152 | tf_op jit(solution)/shard_map/while/body/eval_jaxpr/ppermute | solution.py:14
  348.6 20.6 %collective-permute-start = (f32[1377,256]{1,0:T(8,128)}, f32[1377,256]{1,0:T(8,128)S(1)}, u32[]{:S(2)}, u32[]{:S(2)}) collective-permute-start(f32[1377,256]{1,0:T(8,128)} %get-tuple-element.200), channel_id=1, source_target_pairs={{0,240},{16,0},{32,16},{48,32},{64,48},{80,64},{96,80},{112,96},{1... | collective-permute-start | bytes 4230152 | tf_op jit(solution)/shard_map/while/body/eval_jaxpr/ppermute | solution.py:14
  395.3 12.8 %collective-permute-start.1 = (f32[153,256]{1,0:T(8,128)S(1)}, f32[153,256]{1,0:T(8,128)S(1)}, u32[]{:S(2)}, u32[]{:S(2)}) collective-permute-start(f32[153,256]{1,0:T(8,128)S(1)} %broadcast_multiply_fusion.8), channel_id=1, source_target_pairs={{4,0},{5,1},{6,2},{7,3},{8,4},{9,5},{10,6},{11,7},{12,8},{13,9},{1... | collective-permute-start | bytes 470024 | tf_op jit(solution)/shard_map/ppermute | solution.py:20
  398.1 12.2 %collective-permute-start.2 = (f32[153,256]{1,0:T(8,128)S(1)}, f32[153,256]{1,0:T(8,128)S(1)}, u32[]{:S(2)}, u32[]{:S(2)}) collective-permute-start(f32[153,256]{1,0:T(8,128)S(1)} %broadcast_multiply_fusion.6), channel_id=1, source_target_pairs={{0,4},{1,5},{2,6},{3,7},{4,8},{5,9},{6,10},{7,11},{8,12},{9,13},{1... | collective-permute-start | bytes 470024 | tf_op jit(solution)/shard_map/ppermute | solution.py:20
  414.2 8.9 %collective-permute-start.3 = (f32[153,256]{1,0:T(8,128)S(1)}, f32[153,256]{1,0:T(8,128)S(1)}, u32[]{:S(2)}, u32[]{:S(2)}) collective-permute-start(f32[153,256]{1,0:T(8,128)S(1)} %broadcast_multiply_fusion.4), channel_id=1, source_target_pairs={{1,0},{2,1},{3,2},{4,3},{5,4},{6,5},{7,6},{8,7},{9,8},{10,9},{11,1... | collective-permute-start | bytes 470024 | tf_op jit(solution)/shard_map/ppermute | solution.py:20
  416.3 10.6 %collective-permute-start.4 = (f32[153,256]{1,0:T(8,128)S(1)}, f32[153,256]{1,0:T(8,128)S(1)}, u32[]{:S(2)}, u32[]{:S(2)}) collective-permute-start(f32[153,256]{1,0:T(8,128)S(1)} %broadcast_multiply_fusion.2), channel_id=1, source_target_pairs={{0,1},{1,2},{2,3},{3,4},{4,5},{5,6},{6,7},{7,8},{8,9},{9,10},{10,1... | collective-permute-start | bytes 470024 | tf_op jit(solution)/shard_map/ppermute | solution.py:20
  458.2 13.8 %collective-permute-start.5 = (f32[153,256]{1,0:T(8,128)S(1)}, f32[153,256]{1,0:T(8,128)S(1)}, u32[]{:S(2)}, u32[]{:S(2)}) collective-permute-start(f32[153,256]{1,0:T(8,128)S(1)} %broadcast_multiply_fusion.7), channel_id=1, source_target_pairs={{4,0},{5,1},{6,2},{7,3},{8,4},{9,5},{10,6},{11,7},{12,8},{13,9},{1... | collective-permute-start | bytes 470024 | tf_op jit(solution)/shard_map/ppermute | solution.py:20
  460.1 14.1 %collective-permute-start.6 = (f32[153,256]{1,0:T(8,128)S(1)}, f32[153,256]{1,0:T(8,128)S(1)}, u32[]{:S(2)}, u32[]{:S(2)}) collective-permute-start(f32[153,256]{1,0:T(8,128)S(1)} %broadcast_multiply_fusion.5), channel_id=1, source_target_pairs={{0,4},{1,5},{2,6},{3,7},{4,8},{5,9},{6,10},{7,11},{8,12},{9,13},{1... | collective-permute-start | bytes 470024 | tf_op jit(solution)/shard_map/ppermute | solution.py:20
  478.2 10.2 %collective-permute-start.7 = (f32[153,256]{1,0:T(8,128)S(1)}, f32[153,256]{1,0:T(8,128)S(1)}, u32[]{:S(2)}, u32[]{:S(2)}) collective-permute-start(f32[153,256]{1,0:T(8,128)S(1)} %broadcast_multiply_fusion.3), channel_id=1, source_target_pairs={{1,0},{2,1},{3,2},{4,3},{5,4},{6,5},{7,6},{8,7},{9,8},{10,9},{11,1... | collective-permute-start | bytes 470024 | tf_op jit(solution)/shard_map/ppermute | solution.py:20
  480.1 12.2 %collective-permute-start.8 = (f32[153,256]{1,0:T(8,128)S(1)}, f32[153,256]{1,0:T(8,128)S(1)}, u32[]{:S(2)}, u32[]{:S(2)}) collective-permute-start(f32[153,256]{1,0:T(8,128)S(1)} %broadcast_multiply_fusion.1), channel_id=1, source_target_pairs={{0,1},{1,2},{2,3},{3,4},{4,5},{5,6},{6,7},{7,8},{8,9},{9,10},{10,1... | collective-permute-start | bytes 470024 | tf_op jit(solution)/shard_map/ppermute | solution.py:20
  (6 other events, 24.7 us)
where the time goes:
time: 500 us; the launch traced here: 499 us
  waiting for transfers between devices  257 us (51%)
  starting transfers between devices  91.5 us (18%)
  matrix products  57.4 us (11%)
  other arithmetic  51.3 us (10%)
  local copies, waits for them, and re-layouts  41.3 us (8%)
    ppermute x15, waiting for transfers between devices, from_behind(): lax.ppermute(value, axis, [(i, (i + by) % count) for i in range(count)])  249 us
    ppermute x15, starting transfers between devices, from_behind(): lax.ppermute(value, axis, [(i, (i + by) % count) for i in range(count)])  59.1 us
    dot_general x16, matrix products, matmul(): jnp.dot(left, right, precision=lax.Precision.HIGHEST, preferred_element_t...  45.1 us
    ppermute x8, starting transfers between devices, from_behind_2(): lax.ppermute(value, axis, [(source, source + steps) for source in range(f...  32.4 us
    scatter-add x2, other arithmetic, operator(): jnp.zeros_like(field).at[cell_nodes.reshape(-1)]  17.8 us
    while x15, local copies, waits for them, and re-layouts  16.4 us
    scatter-add x4, other arithmetic, operator(): sectioned.at[shared_rows[2]].add(from_right).at[shared_rows[3]]  15.4 us
    dot_general x2, matrix products, operator(): jnp.einsum('ij,cjs->cis', stiffness[0], gathered, precision=lax.Precision...  12.4 us
  transfers between devices with their start and end apart: 23, of which 17 were waited for; matrix products, arithmetic and copies ran while one was open for 3% of the time, Pallas kernels for 0%

commit v1 on v0

v1 whole, which is shorter than its diff:
```python
import math

import jax
import jax.numpy as jnp
from jax import lax
from jax.sharding import PartitionSpec as P

center_shift = 3.0
half_width = 4.0
SIDE_X = 4
SIDE_Y = 2


def state_id(y, x, core):
    return (y % SIDE_Y) * (SIDE_X * 2) + (x % SIDE_X) * 2 + core % 2


def shift_state(value, dy, dx, dcore):
    pairs = [
        (state_id(y, x, c), state_id(y + dy, x + dx, c + dcore))
        for y in range(SIDE_Y)
        for x in range(SIDE_X)
        for c in range(2)
    ]
    return lax.ppermute(value, "state", pairs)


def shift_mesh(value, steps):
    count = lax.axis_size("mesh")
    first, last = (max(0, -steps), min(count, count - steps))
    return lax.ppermute(value, "mesh", [(source, source + steps) for source in range(first, last)])


def matmul(left, right):
    return jnp.dot(left, right, precision=lax.Precision.HIGH, preferred_element_type=jnp.float32)


def rotate(block, rotation):
    rows, cols = block.shape
    own = lax.axis_index("state")
    y, x, core = own // (SIDE_X * 2), (own // 2) % SIDE_X, own % 2
    chips = rotation.reshape(SIDE_Y * SIDE_X, 2, cols, cols)
    theirs = lax.dynamic_index_in_dim(chips, 1 - core, 1, keepdims=False)
    partner = shift_state(theirs, 0, 0, 1)
    half = rows // 16 * 8

    left = shift_state(block, 0, 1, 0)
    right = shift_state(block, 0, -1, 0)
    across = shift_state(block, 1, 0, 0)
    far_top = shift_state(left[:half], 0, 1, 0)
    far_low = shift_state(right[half:], 0, -1, 0)
    across_left = shift_state(across, 0, 1, 0)
    across_right = shift_state(across, 0, -1, 0)
    across_far_top = shift_state(far_top, 1, 0, 0)
    across_far_low = shift_state(far_low, 1, 0, 0)

    def part(value, dy, dx):
        chip = ((y + dy) % SIDE_Y) * SIDE_X + (x + dx) % SIDE_X
        mine = lax.dynamic_slice_in_dim(rotation, (chip * 2 + core) * cols, cols, 0)
        other = lax.dynamic_index_in_dim(partner, chip, 0, keepdims=False)
        return matmul(value, mine), matmul(value, other)

    def add(a, b):
        return a[0] + b[0], a[1] + b[1]

    total = part(block, 0, 0)
    total = add(total, part(left, 0, -1))
    total = add(total, part(right, 0, 1))
    total = add(total, part(across, 1, 0))
    total = add(total, part(jnp.concatenate([far_top, far_low]), 0, 2))
    total = add(total, part(across_left, 1, -1))
    total = add(total, part(across_right, 1, 1))
    total = add(total, part(jnp.concatenate([across_far_top, across_far_low]), 1, 2))
    return total[0] + shift_state(total[1], 0, 0, 1)


def per_device(states_in, rotation, stiffness, potential, cell_nodes, shared_rows, shared_count):
    block_cols = states_in.shape[1]
    rotated = rotate(states_in, rotation)
    grid_side = math.isqrt(lax.axis_size("mesh"))
    row_mask = (jnp.arange(shared_rows.shape[1])[None, :] < shared_count[0][:, None]).astype(
        jnp.float32
    )

    def trade(values, send_slot, recv_slot, offset):
        block = values[shared_rows[send_slot]] * row_mask[send_slot][:, None]
        arrived = shift_mesh(block, offset)
        return arrived * row_mask[recv_slot][:, None]

    def operator(field):
        gathered = field[cell_nodes]
        product = jnp.einsum("ij,cjs->cis", stiffness[0], gathered, precision=lax.Precision.HIGH)
        local = (
            jnp.zeros_like(field).at[cell_nodes.reshape(-1)].add(product.reshape(-1, block_cols))
        )
        from_next = trade(local, 1, 0, -grid_side)
        from_prev = trade(local, 0, 1, grid_side)
        sectioned = local.at[shared_rows[0]].add(from_next).at[shared_rows[1]].add(from_prev)
        from_right = trade(sectioned, 3, 2, -1)
        from_left = trade(sectioned, 2, 3, 1)
        assembled = sectioned.at[shared_rows[2]].add(from_right).at[shared_rows[3]].add(from_left)
        return assembled + potential[:, None] * field

    current = (operator(rotated) - center_shift * rotated) / half_width
    applied = operator(current)
    following = 2.0 * (applied - center_shift * current) / half_width - rotated
    return following


def solution(mesh):
    return jax.shard_map(
        per_device,
        mesh=mesh,
        in_specs=(
            P("mesh", "state"),
            P(None, "state"),
            P("mesh", None, None),
            P("mesh"),
            P("mesh", None),
            P("mesh", None),
            P("mesh", None),
        ),
        out_specs=P("mesh", "state"),
        check_vma=False,
    )
```

time: 500 us -> 251 us (0.50)
  waiting for transfers between devices: 257 us -> 68.2 us
  starting transfers between devices: 91.5 us -> 46.5 us
  matrix products: 57.4 us -> 39.9 us
  local copies, waits for them, and re-layouts: 41.3 us -> 30.5 us
  other arithmetic: 51.3 us -> 61 us
    ppermute x23 -> x19, waiting for transfers between devices: 257 us -> 68.2 us  [the longest x11 55.5 us: shift_state(): return lax.ppermute(value, 'state', pairs)]
    ppermute x23 -> x19, starting transfers between devices: 91.5 us -> 46.5 us  [the longest x8 32.6 us: shift_mesh(): lax.ppermute(value, 'mesh', [(source, source + steps) for source in range...]
    while x15 -> x0, local copies, waits for them, and re-layouts: 16.4 us -> none
    dot_general x16, matrix products: 45.1 us -> 29.6 us  [matmul(): jnp.dot(left, right, precision=lax.Precision.HIGH, preferred_element_type...]
    scatter-add x4, other arithmetic: 8.82 us -> 18.8 us  [operator(): local.at[shared_rows[0]].add(from_next).at[shared_rows[1]].add(from_prev)]
  transfers between devices with their start and end apart: 23 -> 19, of which waited for: 17 -> 9; matrix products, arithmetic and copies ran while one was open for 3% -> 18% of each run, Pallas kernels for 0% -> 0%
where the time goes in v1:
time: 251 us; the launch traced here: 247 us
  waiting for transfers between devices  68.2 us (27%)
  other arithmetic  61 us (24%)
  starting transfers between devices  46.5 us (19%)
  matrix products  39.9 us (16%)
  local copies, waits for them, and re-layouts  30.5 us (12%)
    ppermute x11, waiting for transfers between devices, shift_state(): return lax.ppermute(value, 'state', pairs)  55.5 us
    ppermute x8, starting transfers between devices, shift_mesh(): lax.ppermute(value, 'mesh', [(source, source + steps) for source in range...  32.6 us
    dot_general x16, matrix products, matmul(): jnp.dot(left, right, precision=lax.Precision.HIGH, preferred_element_type...  29.6 us
    scatter-add x4, other arithmetic, operator(): local.at[shared_rows[0]].add(from_next).at[shared_rows[1]].add(from_prev)  18.8 us
    scatter-add x2, other arithmetic, operator(): jnp.zeros_like(field).at[cell_nodes.reshape(-1)]  17.6 us
    scatter-add x4, other arithmetic, operator(): sectioned.at[shared_rows[2]].add(from_right).at[shared_rows[3]]  15.2 us
    gather x4, local copies, waits for them, and re-layouts, operator(): gathered = field[cell_nodes]  14.6 us
    ppermute x11, starting transfers between devices, shift_state(): return lax.ppermute(value, 'state', pairs)  13.9 us
  transfers between devices with their start and end apart: 19, of which 9 were waited for; matrix products, arithmetic and copies ran while one was open for 18% of the time, Pallas kernels for 0%

profile of v1, /device:TPU:64, one launch (start us, length us, event | category | flops | bytes accessed | tf_op | source)
XLA Modules:
  0.0 246.8 jit_solution(17700124980163332996)
XLA Ops:
  0.0 3.1 %dynamic-slice_bitcast_fusion = f32[8,256,256]{2,1,0:T(8,128)} fusion(f32[8,2,256,256]{3,2,1,0:T(8,128)} %bitcast.105, s32[]{:T(128)S(6)} %select_n.201), kind=kLoop, calls=%fused_computation.47 | loop fusion | bytes 4194308 | tf_op jit(solution)/shard_map/jit(dynamic_index_in_dim)/squeeze | solution.py:43
  11.0 27.0 %collective-permute-done = f32[1377,256]{1,0:T(8,128)S(1)} collective-permute-done((f32[1377,256]{1,0:T(8,128)}, f32[1377,256]{1,0:T(8,128)S(1)}, u32[]{:S(2)}, u32[]{:S(2)}) %collective-permute-start) | collective-permute-done | bytes 1410080 | tf_op jit(solution)/shard_map/ppermute | solution.py:25
  42.4 3.2 %collective-permute-start.6 = (f32[1377,256]{1,0:T(8,128)}, f32[1377,256]{1,0:T(8,128)S(1)}, u32[]{:S(2)}, u32[]{:S(2)}) collective-permute-start(f32[1377,256]{1,0:T(8,128)} %collective-permute-done.2), channel_id=1, source_target_pairs={{0,96},{16,112},{32,0},{48,16},{64,32},{80,48},{96,64},{112,80},{1... | collective-permute-start | bytes 4230152 | tf_op jit(solution)/shard_map/ppermute | solution.py:25
  53.0 5.1 %collective-permute-done.3 = f32[688,256]{1,0:T(8,128)S(1)} collective-permute-done((f32[688,256]{1,0:T(8,128)S(1)}, f32[688,256]{1,0:T(8,128)S(1)}, u32[]{:S(2)}, u32[]{:S(2)}) %collective-permute-start.3) | collective-permute-done | bytes 704544 | tf_op jit(solution)/shard_map/ppermute | solution.py:25
  64.5 12.2 %collective-permute-done.7 = f32[688,256]{1,0:T(8,128)S(1)} collective-permute-done((f32[688,256]{1,0:T(8,128)S(1)}, f32[688,256]{1,0:T(8,128)S(1)}, u32[]{:S(2)}, u32[]{:S(2)}) %collective-permute-start.7) | collective-permute-done | bytes 704544 | tf_op jit(solution)/shard_map/ppermute | solution.py:25
  76.7 10.3 %collective-permute-done.5 = f32[1377,256]{1,0:T(8,128)S(1)} collective-permute-done((f32[1377,256]{1,0:T(8,128)}, f32[1377,256]{1,0:T(8,128)S(1)}, u32[]{:S(2)}, u32[]{:S(2)}) %collective-permute-start.5) | collective-permute-done | bytes 1410080 | tf_op jit(solution)/shard_map/ppermute | solution.py:25
  103.5 4.6 %gather_fusion = f32[1458,256]{1,0:T(8,128)} fusion(f32[1377,256]{1,0:T(8,128)S(1)} %fusion.8, s32[2048]{0:T(1024)S(1)} %pad_clamp_fusion), kind=kCustom, calls=%fused_computation | custom fusion | bytes 2991816 | tf_op jit(solution)/shard_map/gather | solution.py:91
  110.8 5.2 %fusion.20 = f32[2,729,256]{2,1,0:T(8,128)} fusion(f32[2,729,256]{2,1,0:T(8,128)} %reshape.164, f32[1,729,729]{2,0,1:T(1,128)} %param.9), kind=kOutput, calls=%fused_computation.48 | convolution fusion | flops 1632586752 | bytes 5111748 | tf_op jit(solution)/shard_map/ij,cjs->cis/dot_general | solution.py:92
  118.6 8.8 %scatter_custom_fusion = f32[1377,256]{1,0:T(8,128)S(1)} fusion(s32[1458]{0:T(1024)S(1)} %fusion.87, f32[1458,256]{1,0:T(8,128)} %reshape.247, f32[]{:T(128)} %constant.126.clone.1), kind=kCustom, calls=%fused_computation.57 | custom fusion | flops 373248 | bytes 1410560 | tf_op jit(solution)/shard_map/scatter-add | solution.py:94
  128.3 3.3 %collective-permute-start.11 = (f32[153,256]{1,0:T(8,128)S(1)}, f32[153,256]{1,0:T(8,128)S(1)}, u32[]{:S(2)}, u32[]{:S(2)}) collective-permute-start(f32[153,256]{1,0:T(8,128)S(1)} %broadcast_multiply_fusion.8), channel_id=1, source_target_pairs={{4,0},{5,1},{6,2},{7,3},{8,4},{9,5},{10,6},{11,7},{12,8},{13,9},{1... | collective-permute-start | bytes 470024 | tf_op jit(solution)/shard_map/ppermute | solution.py:31
  132.5 5.0 %collective-permute-start.12 = (f32[153,256]{1,0:T(8,128)S(1)}, f32[153,256]{1,0:T(8,128)S(1)}, u32[]{:S(2)}, u32[]{:S(2)}) collective-permute-start(f32[153,256]{1,0:T(8,128)S(1)} %broadcast_multiply_fusion.6), channel_id=1, source_target_pairs={{0,4},{1,5},{2,6},{3,7},{4,8},{5,9},{6,10},{7,11},{8,12},{9,13},{1... | collective-permute-start | bytes 470024 | tf_op jit(solution)/shard_map/ppermute | solution.py:31
  137.6 5.5 %collective-permute-done.11 = f32[153,256]{1,0:T(8,128)S(1)} collective-permute-done((f32[153,256]{1,0:T(8,128)S(1)}, f32[153,256]{1,0:T(8,128)S(1)}, u32[]{:S(2)}, u32[]{:S(2)}) %collective-permute-start.11) | collective-permute-done | bytes 156704 | tf_op jit(solution)/shard_map/ppermute | solution.py:31
  145.3 12.2 %scatter_custom_fusion.2 = f32[1377,256]{1,0:T(8,128)S(1)} fusion(f32[1377,256]{1,0:T(8,128)S(1)} %scatter_custom_fusion.1, s32[153]{0:T(256)S(1)} %bitcast.129, f32[153,256]{1,0:T(8,128)S(1)} %collective-permute-done.12, f32[153]{0:T(256)S(1)} %bitcast.115), kind=kCustom, calls=%fused_computation.104 | custom fusion | flops 78336 | bytes 1574912 | tf_op jit(solution)/shard_map/scatter-add | solution.py:98
  162.3 4.4 %collective-permute-start.14 = (f32[153,256]{1,0:T(8,128)S(1)}, f32[153,256]{1,0:T(8,128)S(1)}, u32[]{:S(2)}, u32[]{:S(2)}) collective-permute-start(f32[153,256]{1,0:T(8,128)S(1)} %broadcast_multiply_fusion.2), channel_id=1, source_target_pairs={{0,1},{1,2},{2,3},{3,4},{4,5},{5,6},{6,7},{7,8},{8,9},{9,10},{10,1... | collective-permute-start | bytes 470024 | tf_op jit(solution)/shard_map/ppermute | solution.py:31
  168.1 3.8 %scatter_custom_fusion.3 = f32[1377,256]{1,0:T(8,128)} fusion(f32[1377,256]{1,0:T(8,128)} %multiply_add_fusion.1, s32[153]{0:T(256)S(1)} %bitcast.126, f32[153,256]{1,0:T(8,128)S(1)} %collective-permute-done.13, f32[153]{0:T(256)S(1)} %bitcast.111), kind=kCustom, calls=%fused_computation.102 | custom fusion | flops 78336 | bytes 1574912 | tf_op jit(solution)/shard_map/scatter-add | solution.py:101
  172.4 3.8 %scatter_custom_fusion.4 = f32[1377,256]{1,0:T(8,128)} fusion(f32[1377,256]{1,0:T(8,128)} %scatter_custom_fusion.3, s32[153]{0:T(256)S(1)} %bitcast.123, f32[153,256]{1,0:T(8,128)S(1)} %collective-permute-done.14, f32[153]{0:T(256)S(1)} %bitcast.107), kind=kCustom, calls=%fused_computation.100 | custom fusion | flops 78336 | bytes 1574912 | tf_op jit(solution)/shard_map/scatter-add | solution.py:101
  177.8 4.6 %gather_fusion.5 = f32[1458,256]{1,0:T(8,128)} fusion(f32[1377,256]{1,0:T(8,128)S(1)} %broadcast_multiply_fusion, s32[2048]{0:T(1024)S(1)} %pad_clamp_fusion), kind=kCustom, calls=%fused_computation.5 | custom fusion | bytes 2991816 | tf_op jit(solution)/shard_map/gather | solution.py:91
  185.1 5.2 %fusion.23 = f32[2,729,256]{2,1,0:T(8,128)} fusion(f32[2,729,256]{2,1,0:T(8,128)} %reshape.204, f32[1,729,729]{2,0,1:T(1,128)} %param.9), kind=kOutput, calls=%fused_computation.49 | convolution fusion | flops 1632586752 | bytes 5111748 | tf_op jit(solution)/shard_map/ij,cjs->cis/dot_general | solution.py:92
  192.9 8.8 %scatter_custom_fusion.5 = f32[1377,256]{1,0:T(8,128)S(1)} fusion(s32[1458]{0:T(1024)S(1)} %fusion.87, f32[1458,256]{1,0:T(8,128)} %reshape.287, f32[]{:T(128)} %constant.126.clone.1), kind=kCustom, calls=%fused_computation.55 | custom fusion | flops 373248 | bytes 1410560 | tf_op jit(solution)/shard_map/scatter-add | solution.py:94
  205.4 7.7 %collective-permute-start.16 = (f32[153,256]{1,0:T(8,128)S(1)}, f32[153,256]{1,0:T(8,128)S(1)}, u32[]{:S(2)}, u32[]{:S(2)}) collective-permute-start(f32[153,256]{1,0:T(8,128)S(1)} %broadcast_multiply_fusion.5), channel_id=1, source_target_pairs={{0,4},{1,5},{2,6},{3,7},{4,8},{5,9},{6,10},{7,11},{8,12},{9,13},{1... | collective-permute-start | bytes 470024 | tf_op jit(solution)/shard_map/ppermute | solution.py:31
  213.2 4.7 %collective-permute-done.15 = f32[153,256]{1,0:T(8,128)S(1)} collective-permute-done((f32[153,256]{1,0:T(8,128)S(1)}, f32[153,256]{1,0:T(8,128)S(1)}, u32[]{:S(2)}, u32[]{:S(2)}) %collective-permute-start.15) | collective-permute-done | bytes 156704 | tf_op jit(solution)/shard_map/ppermute | solution.py:31
  226.0 5.4 %collective-permute-start.18 = (f32[153,256]{1,0:T(8,128)S(1)}, f32[153,256]{1,0:T(8,128)S(1)}, u32[]{:S(2)}, u32[]{:S(2)}) collective-permute-start(f32[153,256]{1,0:T(8,128)S(1)} %broadcast_multiply_fusion.1), channel_id=1, source_target_pairs={{0,1},{1,2},{2,3},{3,4},{4,5},{5,6},{6,7},{7,8},{8,9},{9,10},{10,1... | collective-permute-start | bytes 470024 | tf_op jit(solution)/shard_map/ppermute | solution.py:31
  236.2 3.8 %scatter_custom_fusion.8 = f32[1377,256]{1,0:T(8,128)} fusion(f32[1377,256]{1,0:T(8,128)} %multiply_add_fusion, s32[153]{0:T(256)S(1)} %bitcast.127, f32[153,256]{1,0:T(8,128)S(1)} %collective-permute-done.17, f32[153]{0:T(256)S(1)} %bitcast.113), kind=kCustom, calls=%fused_computation.94 | custom fusion | flops 78336 | bytes 1574912 | tf_op jit(solution)/shard_map/scatter-add | solution.py:101
  240.1 3.8 %scatter_custom_fusion.9 = f32[1377,256]{1,0:T(8,128)} fusion(f32[1377,256]{1,0:T(8,128)} %scatter_custom_fusion.8, s32[153]{0:T(256)S(1)} %bitcast.124, f32[153,256]{1,0:T(8,128)S(1)} %collective-permute-done.18, f32[153]{0:T(256)S(1)} %bitcast.109), kind=kCustom, calls=%fused_computation.92 | custom fusion | flops 78336 | bytes 1574912 | tf_op jit(solution)/shard_map/scatter-add | solution.py:101
  (100 shorter events, 84.4 us)
Async XLA Ops:
  0.0 8.2 %copy-start.3 = (s32[4,153]{1,0:T(4,128)S(1)}, s32[4,153]{1,0:T(4,128)}, u32[]{:S(2)}) copy-start(s32[4,153]{1,0:T(4,128)} %param.12) | copy-start | bytes 7348
  0.0 8.7 %copy-start.6 = (s32[1,4]{1,0:T(1,128)S(1)}, s32[1,4]{1,0:T(1,128)}, u32[]{:S(2)}) copy-start(s32[1,4]{1,0:T(1,128)} %param.13) | copy-start | bytes 52
  3.1 44.2 %collective-permute-start.9 = (f32[8,256,256]{2,1,0:T(8,128)}, f32[8,256,256]{2,1,0:T(8,128)}, u32[]{:S(2)}, u32[]{:S(2)}) collective-permute-start(f32[8,256,256]{2,1,0:T(8,128)} %dynamic-slice_bitcast_fusion), channel_id=1, source_target_pairs={{0,16},{16,0},{32,48},{48,32},{64,80},{80,64},{96,112},{112,96},{1... | collective-permute-start | bytes 6291464 | tf_op jit(solution)/shard_map/ppermute | solution.py:25
  3.1 34.9 %collective-permute-start = (f32[1377,256]{1,0:T(8,128)}, f32[1377,256]{1,0:T(8,128)S(1)}, u32[]{:S(2)}, u32[]{:S(2)}) collective-permute-start(f32[1377,256]{1,0:T(8,128)} %param.7), channel_id=1, source_target_pairs={{0,32},{16,48},{32,64},{48,80},{64,96},{80,112},{96,0},{112,16},{1... | collective-permute-start | bytes 4230152 | tf_op jit(solution)/shard_map/ppermute | solution.py:25
  4.6 37.8 %collective-permute-start.2 = (f32[1377,256]{1,0:T(8,128)}, f32[1377,256]{1,0:T(8,128)}, u32[]{:S(2)}, u32[]{:S(2)}) collective-permute-start(f32[1377,256]{1,0:T(8,128)} %param.7), channel_id=1, source_target_pairs={{0,128},{16,144},{32,160},{48,176},{64,192},{80,208},{96,224},{112... | collective-permute-start | bytes 4230152 | tf_op jit(solution)/shard_map/ppermute | solution.py:25
  6.2 33.1 %collective-permute-start.1 = (f32[1377,256]{1,0:T(8,128)}, f32[1377,256]{1,0:T(8,128)S(1)}, u32[]{:S(2)}, u32[]{:S(2)}) collective-permute-start(f32[1377,256]{1,0:T(8,128)} %param.7), channel_id=1, source_target_pairs={{0,96},{16,112},{32,0},{48,16},{64,32},{80,48},{96,64},{112,80},{1... | collective-permute-start | bytes 4230152 | tf_op jit(solution)/shard_map/ppermute | solution.py:25
  8.2 137.1 %copy-start.4 = (s32[153,1]{0,1:T(1,128)}, s32[153,1]{0,1:T(1,128)S(1)}, u32[]{:S(2)}) copy-start(s32[153,1]{0,1:T(1,128)S(1)} %get-tuple-element.10) | copy-start | bytes 1840
  38.1 19.9 %collective-permute-start.3 = (f32[688,256]{1,0:T(8,128)S(1)}, f32[688,256]{1,0:T(8,128)S(1)}, u32[]{:S(2)}, u32[]{:S(2)}) collective-permute-start(f32[688,256]{1,0:T(8,128)S(1)} %slice.84), channel_id=1, source_target_pairs={{0,32},{16,48},{32,64},{48,80},{64,96},{80,112},{96,0},{112,16},{1... | collective-permute-start | bytes 2113544 | tf_op jit(solution)/shard_map/ppermute | solution.py:25
  39.4 20.3 %collective-permute-start.4 = (f32[689,256]{1,0:T(8,128)S(1)}, f32[689,256]{1,0:T(8,128)S(1)}, u32[]{:S(2)}, u32[]{:S(2)}) collective-permute-start(f32[689,256]{1,0:T(8,128)S(1)} %slice.85), channel_id=1, source_target_pairs={{0,96},{16,112},{32,0},{48,16},{64,32},{80,48},{96,64},{112,80},{1... | collective-permute-start | bytes 2116616 | tf_op jit(solution)/shard_map/ppermute | solution.py:25
  42.4 44.7 %collective-permute-start.5 = (f32[1377,256]{1,0:T(8,128)}, f32[1377,256]{1,0:T(8,128)S(1)}, u32[]{:S(2)}, u32[]{:S(2)}) collective-permute-start(f32[1377,256]{1,0:T(8,128)} %collective-permute-done.2), channel_id=1, source_target_pairs={{0,32},{16,48},{32,64},{48,80},{64,96},{80,112},{96,0},{112,16},{1... | collective-permute-start | bytes 4230152 | tf_op jit(solution)/shard_map/ppermute | solution.py:25
  42.4 48.1 %collective-permute-start.6 = (f32[1377,256]{1,0:T(8,128)}, f32[1377,256]{1,0:T(8,128)S(1)}, u32[]{:S(2)}, u32[]{:S(2)}) collective-permute-start(f32[1377,256]{1,0:T(8,128)} %collective-permute-done.2), channel_id=1, source_target_pairs={{0,96},{16,112},{32,0},{48,16},{64,32},{80,48},{96,64},{112,80},{1... | collective-permute-start | bytes 4230152 | tf_op jit(solution)/shard_map/ppermute | solution.py:25
  58.0 18.7 %collective-permute-start.7 = (f32[688,256]{1,0:T(8,128)S(1)}, f32[688,256]{1,0:T(8,128)S(1)}, u32[]{:S(2)}, u32[]{:S(2)}) collective-permute-start(f32[688,256]{1,0:T(8,128)S(1)} %collective-permute-done.3), channel_id=1, source_target_pairs={{0,128},{16,144},{32,160},{48,176},{64,192},{80,208},{96,224},{112... | collective-permute-start | bytes 2113544 | tf_op jit(solution)/shard_map/ppermute | solution.py:25
  59.7 29.1 %collective-permute-start.8 = (f32[689,256]{1,0:T(8,128)S(1)}, f32[689,256]{1,0:T(8,128)S(1)}, u32[]{:S(2)}, u32[]{:S(2)}) collective-permute-start(f32[689,256]{1,0:T(8,128)S(1)} %collective-permute-done.4), channel_id=1, source_target_pairs={{0,128},{16,144},{32,160},{48,176},{64,192},{80,208},{96,224},{112... | collective-permute-start | bytes 2116616 | tf_op jit(solution)/shard_map/ppermute | solution.py:25
  92.3 9.3 %collective-permute-start.10 = (f32[1377,256]{1,0:T(8,128)S(1)}, f32[1377,256]{1,0:T(8,128)S(1)}, u32[]{:S(2)}, u32[]{:S(2)}) collective-permute-start(f32[1377,256]{1,0:T(8,128)S(1)} %fusion.4), channel_id=1, source_target_pairs={{0,16},{16,0},{32,48},{48,32},{64,80},{80,64},{96,112},{112,96},{1... | collective-permute-start | bytes 4230152 | tf_op jit(solution)/shard_map/ppermute | solution.py:25
  128.3 14.8 %collective-permute-start.11 = (f32[153,256]{1,0:T(8,128)S(1)}, f32[153,256]{1,0:T(8,128)S(1)}, u32[]{:S(2)}, u32[]{:S(2)}) collective-permute-start(f32[153,256]{1,0:T(8,128)S(1)} %broadcast_multiply_fusion.8), channel_id=1, source_target_pairs={{4,0},{5,1},{6,2},{7,3},{8,4},{9,5},{10,6},{11,7},{12,8},{13,9},{1... | collective-permute-start | bytes 470024 | tf_op jit(solution)/shard_map/ppermute | solution.py:31
  132.5 12.8 %collective-permute-start.12 = (f32[153,256]{1,0:T(8,128)S(1)}, f32[153,256]{1,0:T(8,128)S(1)}, u32[]{:S(2)}, u32[]{:S(2)}) collective-permute-start(f32[153,256]{1,0:T(8,128)S(1)} %broadcast_multiply_fusion.6), channel_id=1, source_target_pairs={{0,4},{1,5},{2,6},{3,7},{4,8},{5,9},{6,10},{7,11},{8,12},{9,13},{1... | collective-permute-start | bytes 470024 | tf_op jit(solution)/shard_map/ppermute | solution.py:31
  158.3 8.4 %copy-start.1 = (f32[1377]{0:T(1024)S(1)}, f32[1377]{0:T(1024)}, u32[]{:S(2)}) copy-start(f32[1377]{0:T(1024)} %param.10) | copy-start | bytes 16528
  158.4 9.7 %collective-permute-start.13 = (f32[153,256]{1,0:T(8,128)S(1)}, f32[153,256]{1,0:T(8,128)S(1)}, u32[]{:S(2)}, u32[]{:S(2)}) collective-permute-start(f32[153,256]{1,0:T(8,128)S(1)} %broadcast_multiply_fusion.4), channel_id=1, source_target_pairs={{1,0},{2,1},{3,2},{4,3},{5,4},{6,5},{7,6},{8,7},{9,8},{10,9},{11,1... | collective-permute-start | bytes 470024 | tf_op jit(solution)/shard_map/ppermute | solution.py:31
  162.3 10.2 %collective-permute-start.14 = (f32[153,256]{1,0:T(8,128)S(1)}, f32[153,256]{1,0:T(8,128)S(1)}, u32[]{:S(2)}, u32[]{:S(2)}) collective-permute-start(f32[153,256]{1,0:T(8,128)S(1)} %broadcast_multiply_fusion.2), channel_id=1, source_target_pairs={{0,1},{1,2},{2,3},{3,4},{4,5},{5,6},{6,7},{7,8},{8,9},{9,10},{10,1... | collective-permute-start | bytes 470024 | tf_op jit(solution)/shard_map/ppermute | solution.py:31
  203.4 14.5 %collective-permute-start.15 = (f32[153,256]{1,0:T(8,128)S(1)}, f32[153,256]{1,0:T(8,128)S(1)}, u32[]{:S(2)}, u32[]{:S(2)}) collective-permute-start(f32[153,256]{1,0:T(8,128)S(1)} %broadcast_multiply_fusion.7), channel_id=1, source_target_pairs={{4,0},{5,1},{6,2},{7,3},{8,4},{9,5},{10,6},{11,7},{12,8},{13,9},{1... | collective-permute-start | bytes 470024 | tf_op jit(solution)/shard_map/ppermute | solution.py:31
  205.4 14.6 %collective-permute-start.16 = (f32[153,256]{1,0:T(8,128)S(1)}, f32[153,256]{1,0:T(8,128)S(1)}, u32[]{:S(2)}, u32[]{:S(2)}) collective-permute-start(f32[153,256]{1,0:T(8,128)S(1)} %broadcast_multiply_fusion.5), channel_id=1, source_target_pairs={{0,4},{1,5},{2,6},{3,7},{4,8},{5,9},{6,10},{7,11},{8,12},{9,13},{1... | collective-permute-start | bytes 470024 | tf_op jit(solution)/shard_map/ppermute | solution.py:31
  224.0 12.2 %collective-permute-start.17 = (f32[153,256]{1,0:T(8,128)S(1)}, f32[153,256]{1,0:T(8,128)S(1)}, u32[]{:S(2)}, u32[]{:S(2)}) collective-permute-start(f32[153,256]{1,0:T(8,128)S(1)} %broadcast_multiply_fusion.3), channel_id=1, source_target_pairs={{1,0},{2,1},{3,2},{4,3},{5,4},{6,5},{7,6},{8,7},{9,8},{10,9},{11,1... | collective-permute-start | bytes 470024 | tf_op jit(solution)/shard_map/ppermute | solution.py:31
  226.0 14.0 %collective-permute-start.18 = (f32[153,256]{1,0:T(8,128)S(1)}, f32[153,256]{1,0:T(8,128)S(1)}, u32[]{:S(2)}, u32[]{:S(2)}) collective-permute-start(f32[153,256]{1,0:T(8,128)S(1)} %broadcast_multiply_fusion.1), channel_id=1, source_target_pairs={{0,1},{1,2},{2,3},{3,4},{4,5},{5,6},{6,7},{7,8},{8,9},{9,10},{10,1... | collective-permute-start | bytes 470024 | tf_op jit(solution)/shard_map/ppermute | solution.py:31
  234.3 9.6 %copy-start = (f32[1377,256]{1,0:T(8,128)S(1)}, f32[1377,256]{1,0:T(8,128)}, u32[]{:S(2)}) copy-start(f32[1377,256]{1,0:T(8,128)} %scatter_custom_fusion.4) | copy-start | bytes 4230148
  (2 other events, 8.5 us)
